TPU v7x, 256 devices: a whole 4x4x8 slice. The times are simulated.
256 devices in a mesh: branch: 2 (over core), seq: 8 (over y, x_hi), rep: 16 (over z, x_lo).
Axes of the slice: x: 4 (x_hi: 2, x_lo: 2; x = x_hi * 2 + x_lo), y: 4, z: 8, core: 2. Of those that a mesh axis runs over, the one named last changes fastest.
Arguments:
- queries: bfloat16 [2, 16384, 2048], P('branch', ('rep', 'seq')), parts along dimension 1, may hold values from -64 to 64
- key_vecs: bfloat16 [2, 16384, 2048], P('branch', ('rep', 'seq')), parts along dimension 1, may hold values from -8 to 8
- value_vecs: bfloat16 [2, 16384, 2048], P('branch', ('rep', 'seq')), parts along dimension 1, may hold values from -6 to 6
- hidden_in: bfloat16 [2, 16384, 2048], P('branch', ('rep', 'seq')), parts along dimension 1, may hold values from -4 to 4
- out_proj: bfloat16 [2, 2048, 2048], P('branch', 'seq'), may hold values from -0.125 to 0.125
- couple_proj: bfloat16 [2, 2048, 2048], P('branch', 'seq'), may hold values from -0.125 to 0.125
- grad_mixed: bfloat16 [2, 16384, 2048], P('branch', ('rep', 'seq')), parts along dimension 1, may hold values from -6 to 6
Outputs:
- mixed_out: bfloat16 [2, 16384, 2048], P('branch', ('rep', 'seq')), parts along dimension 1
- grad_hidden: bfloat16 [2, 16384, 2048], P('branch', ('rep', 'seq')), parts along dimension 1
- grad_queries: bfloat16 [2, 16384, 2048], P('branch', ('rep', 'seq')), parts along dimension 1
- grad_keys: bfloat16 [2, 16384, 2048], P('branch', ('rep', 'seq')), parts along dimension 1
- grad_values: bfloat16 [2, 16384, 2048], P('branch', ('rep', 'seq')), parts along dimension 1
- grad_couple: float32 [2, 2048, 32768], P('branch', 'seq', 'rep'), parts along dimension 2
There are 16 independent parts, one for each index of `rep`. A program takes and returns all parts, laid end to end along the dimension named above; an argument that names none is the same for every part. Nothing has to cross between parts.
All inputs are finite; a program needn't handle non-finite values.
Results may differ from a plain program's by a relative error of at most 0.015.
Values may be sent and summed in bfloat16 or wider, within the bound.
No kernel may reach another device: no remote copies, remote signals or barrier semaphores. Data moves between devices by JAX's collectives and lax.ppermute only.
A program may use at most 128 MiB of HBM per device.

v0:
```python
import math
import jax
import jax.numpy as jnp
from jax import lax
from jax.sharding import PartitionSpec as P

HEAD = 128


def swapped(value, axis, bit):
    mask = 2**bit
    pairs = [(source, source ^ mask) for source in range(lax.axis_size(axis))]
    return lax.ppermute(value, axis, pairs)


def contract(left, right, left_dim, right_dim):
    return lax.dot_general(
        left, right, (((left_dim,), (right_dim,)), ((), ())), preferred_element_type=jnp.float32
    )


def softmax_weights(query_item, key_item, factor):
    scores = contract(query_item, key_item, 1, 1) * factor
    row_max = jnp.max(scores, axis=-1, keepdims=True)
    raised = jnp.exp(scores - row_max)
    return raised / jnp.sum(raised, axis=-1, keepdims=True)


def forward_item(bundle, factor):
    query_item, key_item, value_item = bundle
    weights = softmax_weights(query_item, key_item, factor)
    return contract(weights.astype(jnp.bfloat16), value_item, 1, 0).astype(jnp.bfloat16)


def backward_item(bundle, factor):
    query_item, key_item, value_item, grad_item = bundle
    weights = softmax_weights(query_item, key_item, factor)
    weights_low = weights.astype(jnp.bfloat16)
    grad_weights = contract(grad_item, value_item, 1, 1)
    row_dot = jnp.sum(weights * grad_weights, axis=-1, keepdims=True)
    d_scores = (weights * (grad_weights - row_dot)).astype(jnp.bfloat16)
    grad_query = (contract(d_scores, key_item, 1, 0) * factor).astype(jnp.bfloat16)
    grad_key = (contract(d_scores, query_item, 0, 0) * factor).astype(jnp.bfloat16)
    grad_value = contract(weights_low, grad_item, 0, 0).astype(jnp.bfloat16)
    return (grad_query, grad_key, grad_value)


def head_items(block_rows, seq_len):
    groups = block_rows.shape[0] // seq_len
    heads_here = block_rows.shape[1] // HEAD
    return (
        block_rows.reshape(groups, seq_len, heads_here, HEAD)
        .transpose(0, 2, 1, 3)
        .reshape(groups * heads_here, seq_len, HEAD)
    )


def item_rows(items, groups):
    heads_here = items.shape[0] // groups
    seq_len = items.shape[1]
    return (
        items.reshape(groups, heads_here, seq_len, HEAD)
        .transpose(0, 2, 1, 3)
        .reshape(groups * seq_len, heads_here * HEAD)
    )


def grouped_product(attended, projection, group_count):
    tok_rows = attended.shape[0]
    width = attended.shape[1] // group_count
    left = attended.reshape(tok_rows, group_count, width)
    right = projection.reshape(group_count, width, projection.shape[1])
    product = lax.dot_general(
        left, right, (((2,), (1,)), ((1,), (0,))), preferred_element_type=jnp.float32
    )
    rounded = lax.optimization_barrier(product.astype(jnp.bfloat16))
    return jnp.sum(rounded.astype(jnp.float32), axis=0)


def on_device(queries, key_vecs, value_vecs, hidden_in, out_proj, couple_proj, grad_mixed):
    factor = 1.0 / math.sqrt(HEAD)
    tok_count = queries.shape[1]
    group_count = lax.axis_size("seq")
    seq_len = tok_count * group_count
    head_query, head_key, head_value = (
        lax.all_to_all(queries[0], ("branch", "seq"), split_axis=1, concat_axis=0, tiled=True),
        lax.all_to_all(key_vecs[0], ("branch", "seq"), split_axis=1, concat_axis=0, tiled=True),
        lax.all_to_all(value_vecs[0], ("branch", "seq"), split_axis=1, concat_axis=0, tiled=True),
    )
    groups = head_query.shape[0] // seq_len
    query_items = head_items(head_query, seq_len)
    key_items = head_items(head_key, seq_len)
    value_items = head_items(head_value, seq_len)
    attended_items = lax.map(
        lambda bundle: forward_item(bundle, factor), (query_items, key_items, value_items)
    )
    attended_rows = item_rows(attended_items, groups)
    attended = lax.all_to_all(
        attended_rows, ("branch", "seq"), split_axis=0, concat_axis=1, tiled=True
    )
    proj_own = lax.all_gather(out_proj, "seq", axis=1, tiled=True)[0]
    summed = hidden_in[0].astype(jnp.float32) + grouped_product(attended, proj_own, group_count)
    hidden = lax.optimization_barrier(summed.astype(jnp.bfloat16))
    partner = swapped(hidden, "branch", 0)
    couple_full = lax.all_gather(couple_proj, "seq", axis=1, tiled=True)[0]
    mixed_out = (hidden.astype(jnp.float32) + contract(partner, couple_full, 1, 0)).astype(
        jnp.bfloat16
    )
    grad_tok = grad_mixed[0]
    back_couple = contract(grad_tok, couple_full, 1, 1).astype(jnp.bfloat16)
    partner_back = swapped(back_couple, "branch", 0)
    grad_hid = (grad_tok.astype(jnp.float32) + partner_back.astype(jnp.float32)).astype(
        jnp.bfloat16
    )
    grad_attended = contract(grad_hid, proj_own, 1, 1).astype(jnp.bfloat16)
    head_grad = lax.all_to_all(
        grad_attended, ("branch", "seq"), split_axis=1, concat_axis=0, tiled=True
    )
    grad_cpl = lax.psum_scatter(
        contract(partner, grad_tok, 0, 0).astype(jnp.bfloat16),
        "seq",
        scatter_dimension=0,
        tiled=True,
    ).astype(jnp.float32)
    grad_items = lax.map(
        lambda bundle: backward_item(bundle, factor),
        (query_items, key_items, value_items, head_items(head_grad, seq_len)),
    )
    back_rows = (
        item_rows(grad_items[0], groups),
        item_rows(grad_items[1], groups),
        item_rows(grad_items[2], groups),
    )
    grad_q, grad_k, grad_v = (
        lax.all_to_all(back_rows[0], ("branch", "seq"), split_axis=0, concat_axis=1, tiled=True),
        lax.all_to_all(back_rows[1], ("branch", "seq"), split_axis=0, concat_axis=1, tiled=True),
        lax.all_to_all(back_rows[2], ("branch", "seq"), split_axis=0, concat_axis=1, tiled=True),
    )
    return (
        mixed_out[None],
        grad_hid[None],
        grad_q[None],
        grad_k[None],
        grad_v[None],
        grad_cpl[None],
    )


def solution(mesh):
    return jax.shard_map(
        on_device,
        mesh=mesh,
        in_specs=(
            P("branch", ("rep", "seq"), None),
            P("branch", ("rep", "seq"), None),
            P("branch", ("rep", "seq"), None),
            P("branch", ("rep", "seq"), None),
            P("branch", "seq", None),
            P("branch", "seq", None),
            P("branch", ("rep", "seq"), None),
        ),
        out_specs=(
            P("branch", ("rep", "seq"), None),
            P("branch", ("rep", "seq"), None),
            P("branch", ("rep", "seq"), None),
            P("branch", ("rep", "seq"), None),
            P("branch", ("rep", "seq"), None),
            P("branch", "seq", "rep"),
        ),
        check_vma=False,
    )
```

profile of v0, /device:TPU:1, one launch (start us, length us, event | category | flops | bytes accessed | tf_op | source)
XLA Modules:
  0.0 394.4 jit_solution(10062124970010000764)
XLA Ops:
  7.2 0.7 all-gather.3.cloned.1.call-update
  8.0 0.7 all-gather.5.cloned.1.call-update
  8.7 1.1 copy.57
  9.8 0.9 copy.43
  10.8 8.4 %all-to-all-start = ((bf16[128,16,128]{2,0,1:T(8,128)(2,1)}), bf16[128,16,128]{2,0,1:T(8,128)(2,1)S(1)}, u32[]{:S(2)}, u32[]{:S(2)}) async-start(bf16[128,16,128]{2,0,1:T(8,128)(2,1)} %copy.43), calls=%async_computation | async-start | bytes 1048576 | tf_op jit(solution)/shard_map/all_to_all | solution.py:86
  19.3 0.9 copy.44
  20.3 9.0 %all-to-all-done = bf16[128,16,128]{2,0,1:T(8,128)(2,1)S(1)} async-done(((bf16[128,16,128]{2,0,1:T(8,128)(2,1)}), bf16[128,16,128]{2,0,1:T(8,128)(2,1)S(1)}, u32[]{:S(2)}, u32[]{:S(2)}) %all-to-all-start) | async-done | bytes 524320 | tf_op jit(solution)/shard_map/all_to_all | solution.py:86
  29.3 5.2 %all-to-all-start.1 = ((bf16[128,16,128]{2,0,1:T(8,128)(2,1)}), bf16[128,16,128]{2,0,1:T(8,128)(2,1)S(1)}, u32[]{:S(2)}, u32[]{:S(2)}) async-start(bf16[128,16,128]{2,0,1:T(8,128)(2,1)} %copy.44), calls=%async_computation.1 | async-start | bytes 1048576 | tf_op jit(solution)/shard_map/all_to_all | solution.py:87
  34.6 0.9 copy.45
  35.5 13.9 %all-to-all-done.1 = bf16[128,16,128]{2,0,1:T(8,128)(2,1)S(1)} async-done(((bf16[128,16,128]{2,0,1:T(8,128)(2,1)}), bf16[128,16,128]{2,0,1:T(8,128)(2,1)S(1)}, u32[]{:S(2)}, u32[]{:S(2)}) %all-to-all-start.1) | async-done | bytes 524320 | tf_op jit(solution)/shard_map/all_to_all | solution.py:87
  49.4 4.6 %all-to-all-start.2 = ((bf16[128,16,128]{2,0,1:T(8,128)(2,1)}), bf16[128,16,128]{2,0,1:T(8,128)(2,1)S(1)}, u32[]{:S(2)}, u32[]{:S(2)}) async-start(bf16[128,16,128]{2,0,1:T(8,128)(2,1)} %copy.45), calls=%async_computation.2 | async-start | bytes 1048576 | tf_op jit(solution)/shard_map/all_to_all | solution.py:88
  54.0 10.0 %all-to-all-done.2 = bf16[128,16,128]{2,0,1:T(8,128)(2,1)S(1)} async-done(((bf16[128,16,128]{2,0,1:T(8,128)(2,1)}), bf16[128,16,128]{2,0,1:T(8,128)(2,1)S(1)}, u32[]{:S(2)}, u32[]{:S(2)}) %all-to-all-start.2) | async-done | bytes 524320 | tf_op jit(solution)/shard_map/all_to_all | solution.py:88
  64.1 5.4 %while.24 = (s32[]{:T(128)}, bf16[2,1024,128]{2,1,0:T(8,128)(2,1)S(1)}, bf16[2,1024,128]{2,1,0:T(8,128)(2,1)S(1)}, bf16[2,1024,128]{2,1,0:T(8,128)(2,1)S(1)}, bf16[2,1024,128]{2,1,0:T(8,128)(2,1)S(1)}, /*index=5*/s32[]{:T(128)}) while((s32[]{:T(128)}, bf16[2,1024,128]{2,1,0:T(8,128)(2,1)S(1)}, bf16[2,1024,128]{2,1,0:T(8,128)(2,1)S(1)}, ...), condition=%wide.region_3.4_spmd, body=%wide.region_0.3_spmd.sunk | while | flops 546437120 | bytes 13654085 | solution.py:94
  64.1 0.7 multiply_reduce_fusion.6
  64.9 0.7 fusion.104
  65.6 1.2 fusion.105
  66.8 0.7 multiply_reduce_fusion.6
  67.6 0.7 fusion.104
  68.3 1.3 fusion.105
  69.6 0.8 copy-done.8
  70.4 20.5 %all_to_all.128 = bf16[16,128,128]{2,1,0:T(8,128)(2,1)S(1)} all-to-all(bf16[16,128,128]{2,1,0:T(8,128)(2,1)S(1)} %bitcast.181), channel_id=1, replica_groups=mesh['branch'=2,'seq'=8,'rep'=16] {'branch','seq'}, dimensions={0} | all-to-all | bytes 1048576 | tf_op jit(solution)/shard_map/all_to_all | solution.py:98
  91.2 43.9 %all-gather.3.cloned.1.call-done = bf16[1,2048,2048]{2,1,0:T(8,128)(2,1)} async-done(((bf16[1,256,2048]{2,1,0:T(8,128)(2,1)}), bf16[1,2048,2048]{2,1,0:T(8,128)(2,1)}) %all-gather.3.cloned.1.call-update) | async-done | bytes 8388624 | tf_op jit(solution)/shard_map/all_gather | solution.py:101
  135.0 4.7 %convolution_convert_fusion.1 = bf16[8,128,2048]{2,1,0:T(8,128)(2,1)S(1)} fusion(bf16[128,8,256]{0,2,1:T(8,128)(2,1)S(1)} %bitcast.177, bf16[8,256,2048]{2,1,0:T(8,128)(2,1)} %bitcast.174), kind=kOutput, calls=%fused_computation.66 | convolution fusion | flops 1075838976 | bytes 13107200 | tf_op jit(solution)/shard_map/dot_general | solution.py:73
  139.8 0.7 convert_reduce_fusion
  140.9 0.8 copy-done.5
  141.7 1.4 collective-permute-start
  143.1 1.5 collective-permute-done
  144.6 6.0 %convolution_convert_fusion = bf16[2048,2048]{1,0:T(8,128)(2,1)} fusion(bf16[128,2048]{1,0:T(8,128)(2,1)S(1)} %collective-permute-done, bf16[1,128,2048]{2,1,0:T(8,128)(2,1)S(1)} %copy-done), kind=kOutput, calls=%fused_computation.65 | convolution fusion | flops 1077936128 | bytes 9437184 | tf_op jit(solution)/shard_map/dot_general | solution.py:17
  150.6 96.6 %all-gather.5.cloned.1.call-done = bf16[1,2048,2048]{2,1,0:T(8,128)(2,1)} async-done(((bf16[1,256,2048]{2,1,0:T(8,128)(2,1)}), bf16[1,2048,2048]{2,1,0:T(8,128)(2,1)}) %all-gather.5.cloned.1.call-update) | async-done | bytes 8388624 | tf_op jit(solution)/shard_map/all_gather | solution.py:105
  247.2 6.2 %fusion.65 = bf16[128,2048]{1,0:T(8,128)(2,1)S(1)} fusion(bf16[1,2048,2048]{2,1,0:T(8,128)(2,1)} %all-gather.5.cloned.1.call-done, bf16[1,128,2048]{2,1,0:T(8,128)(2,1)S(1)} %copy-done), kind=kOutput, calls=%fused_computation.68 | convolution fusion | flops 1074003968 | bytes 9437184 | tf_op jit(solution)/shard_map/dot_general | solution.py:17
  253.5 1.7 collective-permute-start.1
  255.2 1.5 collective-permute-done.1
  256.7 6.3 %fusion.77 = bf16[16,16,8,128]{3,2,1,0:T(8,128)(2,1)S(1)} fusion(bf16[1,2048,2048]{2,1,0:T(8,128)(2,1)} %all-gather.3.cloned.1.call-done, bf16[128,2048]{1,0:T(8,128)(2,1)S(1)} %collective-permute-done.1, bf16[1,128,2048]{2,1,0:T(8,128)(2,1)S(1)} %copy-done), kind=kOutput, calls=%fused_computation.72 | convolution fusion | flops 1075052544 | bytes 9961472 | tf_op jit(solution)/shard_map/dot_general | solution.py:17
  263.1 18.9 %all_to_all.131 = bf16[128,16,128]{2,0,1:T(8,128)(2,1)} all-to-all(bf16[128,16,128]{2,0,1:T(8,128)(2,1)S(1)} %bitcast.183), channel_id=1, replica_groups=mesh['branch'=2,'seq'=8,'rep'=16] {'branch','seq'}, dimensions={1} | all-to-all | bytes 1048576 | tf_op jit(solution)/shard_map/all_to_all | solution.py:116
  282.1 0.9 broadcast.17.clone.2
  283.0 0.9 broadcast.17.clone.3
  283.8 14.7 %while.25 = (s32[]{:T(128)}, bf16[2,1024,128]{2,1,0:T(8,128)(2,1)S(1)}, bf16[2,1024,128]{2,1,0:T(8,128)(2,1)}, bf16[2,1024,128]{2,1,0:T(8,128)(2,1)}, bf16[2,102...) while((s32[]{:T(128)}, ...), condition=%wide.region_9.10_spmd, body=%wide.region_5.9_spmd.sunk | while | flops 1363801088 | bytes 50906372 | solution.py:125
  283.8 0.7 multiply_reduce_fusion.7
  284.5 0.7 fusion.112
  285.3 1.0 fusion.115
  286.4 1.1 multiply_reduce_fusion.8
  287.5 1.2 multiply_convert_fusion.2
  288.7 0.8 fusion.114
  289.5 0.8 copy-done.2
  290.3 0.9 fusion.113
  291.2 0.7 multiply_reduce_fusion.7
  291.9 0.7 fusion.112
  292.7 1.0 fusion.115
  293.8 1.1 multiply_reduce_fusion.8
  294.9 1.2 multiply_convert_fusion.2
  296.1 0.8 fusion.114
  296.9 0.8 copy-done.2
  297.7 0.9 fusion.113
  298.6 19.4 %all_to_all.129 = bf16[16,128,128]{2,1,0:T(8,128)(2,1)S(1)} all-to-all(bf16[16,128,128]{2,1,0:T(8,128)(2,1)S(1)} %bitcast.178), channel_id=1, replica_groups=mesh['branch'=2,'seq'=8,'rep'=16] {'branch','seq'}, dimensions={0} | all-to-all | bytes 1048576 | tf_op jit(solution)/shard_map/all_to_all | solution.py:135
  318.0 19.9 %all_to_all.130 = bf16[16,128,128]{2,1,0:T(8,128)(2,1)S(1)} all-to-all(bf16[16,128,128]{2,1,0:T(8,128)(2,1)} %bitcast.179), channel_id=1, replica_groups=mesh['branch'=2,'seq'=8,'rep'=16] {'branch','seq'}, dimensions={0} | all-to-all | bytes 1048576 | tf_op jit(solution)/shard_map/all_to_all | solution.py:136
  337.9 5.9 %all-to-all-start.7 = ((bf16[16,128,128]{2,1,0:T(8,128)(2,1)}), bf16[16,128,128]{2,1,0:T(8,128)(2,1)S(1)}, u32[]{:S(2)}, u32[]{:S(2)}) async-start(bf16[16,128,128]{2,1,0:T(8,128)(2,1)} %bitcast.180), calls=%async_computation.7 | async-start | bytes 1048576 | tf_op jit(solution)/shard_map/all_to_all | solution.py:137
  343.7 5.6 %fusion.74 = bf16[1,128,2048]{2,1,0:T(8,128)(2,1)} fusion(bf16[128,2048]{1,0:T(8,128)(2,1)S(1)} %collective-permute-done, bf16[1,2048,2048]{2,1,0:T(8,128)(2,1)} %all-gather.5.cloned.1.call-done, bf16[128,2048]{1,0:T(8,128)(2,1)} %copy-done.5), kind=kOutput, calls=%fused_computation.71 | convolution fusion | flops 1074528256 | bytes 9961472 | tf_op jit(solution)/shard_map/dot_general | solution.py:17
  349.3 0.9 fusion.83
  350.5 1.0 copy.52
  351.8 1.0 copy.53
  352.8 1.0 all-to-all-done.7
  354.1 1.0 copy.54
  355.1 30.0 %reduce-scatter.2.cloned.1.call-done = bf16[256,2048]{1,0:T(8,128)(2,1)} async-done(((bf16[2048,2048]{1,0:T(8,128)(2,1)}), bf16[256,2048]{1,0:T(8,128)(2,1)}) %reduce-scatter.2.cloned.1.call-update) | async-done | bytes 1048592 | tf_op jit(solution)/shard_map/reduce_scatter | solution.py:119
  385.1 2.8 bitcast_convert_fusion
  (46 shorter events, 2.3 us)
Async XLA Ops:
  7.2 12.0 %copy-start.6 = (bf16[1,128,2048]{2,1,0:T(8,128)(2,1)S(1)}, bf16[1,128,2048]{2,1,0:T(8,128)(2,1)}, u32[]{:S(2)}) copy-start(bf16[1,128,2048]{2,1,0:T(8,128)(2,1)} %param.12) | copy-start | bytes 1572868
  7.2 27.3 %copy-start.7 = (bf16[1,128,2048]{2,1,0:T(8,128)(2,1)S(1)}, bf16[1,128,2048]{2,1,0:T(8,128)(2,1)}, u32[]{:S(2)}) copy-start(bf16[1,128,2048]{2,1,0:T(8,128)(2,1)} %param.13) | copy-start | bytes 1572868
  7.2 127.8 %all-gather.3.cloned.1.call-start = ((), (), s32[]{:S(2)}) async-start(), calls=%async_computation.9 | async-start | bytes 9437184 | tf_op jit(solution)/shard_map/all_gather | solution.py:101
  7.9 239.3 %all-gather.5.cloned.1.call-start = ((), (), s32[]{:S(2)}) async-start(), calls=%async_computation.10 | async-start | bytes 9437184 | tf_op jit(solution)/shard_map/all_gather | solution.py:105
  10.8 18.5 %all-to-all-start = ((bf16[128,16,128]{2,0,1:T(8,128)(2,1)}), bf16[128,16,128]{2,0,1:T(8,128)(2,1)S(1)}, u32[]{:S(2)}, u32[]{:S(2)}) async-start(bf16[128,16,128]{2,0,1:T(8,128)(2,1)} %copy.43), calls=%async_computation | async-start | bytes 1048576 | tf_op jit(solution)/shard_map/all_to_all | solution.py:86
  29.3 20.2 %all-to-all-start.1 = ((bf16[128,16,128]{2,0,1:T(8,128)(2,1)}), bf16[128,16,128]{2,0,1:T(8,128)(2,1)S(1)}, u32[]{:S(2)}, u32[]{:S(2)}) async-start(bf16[128,16,128]{2,0,1:T(8,128)(2,1)} %copy.44), calls=%async_computation.1 | async-start | bytes 1048576 | tf_op jit(solution)/shard_map/all_to_all | solution.py:87
  49.4 14.6 %all-to-all-start.2 = ((bf16[128,16,128]{2,0,1:T(8,128)(2,1)}), bf16[128,16,128]{2,0,1:T(8,128)(2,1)S(1)}, u32[]{:S(2)}, u32[]{:S(2)}) async-start(bf16[128,16,128]{2,0,1:T(8,128)(2,1)} %copy.45), calls=%async_computation.2 | async-start | bytes 1048576 | tf_op jit(solution)/shard_map/all_to_all | solution.py:88
  54.0 331.1 %reduce-scatter.2.cloned.1.call-start = ((), (), s32[]{:S(2)}) async-start(), calls=%async_computation.11 | async-start | bytes 9437184 | tf_op jit(solution)/shard_map/reduce_scatter | solution.py:119
  69.6 0.8 copy-start.8
  139.7 1.0 copy-start.11
  139.8 4.9 %copy-start = (bf16[1,128,2048]{2,1,0:T(8,128)(2,1)S(1)}, bf16[1,128,2048]{2,1,0:T(8,128)(2,1)}, u32[]{:S(2)}) copy-start(bf16[1,128,2048]{2,1,0:T(8,128)(2,1)} %param.17) | copy-start | bytes 1572868
  140.9 0.8 copy-start.5
  141.7 2.9 collective-permute-start
  253.5 3.2 collective-permute-start.1
  283.8 1.5 copy-start.3
  283.8 1.5 copy-start.10
  285.3 1.1 copy-start.9
  286.3 1.1 copy-start.4
  287.5 1.2 copy-start.1
  289.5 0.8 copy-start.2
  291.2 1.5 copy-start.3
  291.2 1.5 copy-start.10
  292.7 1.1 copy-start.9
  293.7 1.1 copy-start.4
  294.9 1.2 copy-start.1
  296.9 0.8 copy-start.2
  337.9 15.9 %all-to-all-start.7 = ((bf16[16,128,128]{2,1,0:T(8,128)(2,1)}), bf16[16,128,128]{2,1,0:T(8,128)(2,1)S(1)}, u32[]{:S(2)}, u32[]{:S(2)}) async-start(bf16[16,128,128]{2,1,0:T(8,128)(2,1)} %bitcast.180), calls=%async_computation.7 | async-start | bytes 1048576 | tf_op jit(solution)/shard_map/all_to_all | solution.py:137
Sparse Core Ops, SparseCore 0:
  10.6 124.3 all-gather.2
  137.7 109.5 all-gather.4
  251.3 133.7 reduce-scatter.1
where the time goes:
time: 395 us; the launch traced here: 394 us
  waiting for transfers between devices  209 us (53%)
  blocking collectives  78.7 us (20%)
  matrix products  41.7 us (11%)
  starting transfers between devices  27.3 us (7%)
  local copies, waits for them, and re-layouts  13.9 us (4%)
  between operations  13.9 us (4%)
  other arithmetic  9.85 us (2%)
    all_gather x1, waiting for transfers between devices, on_device(): couple_full = lax.all_gather(couple_proj, 'seq', axis=1, tiled=True)[0]  96.6 us
    all_gather x1, waiting for transfers between devices, on_device(): proj_own = lax.all_gather(out_proj, 'seq', axis=1, tiled=True)[0]  43.9 us
    dot_general x18, matrix products, contract(): lax.dot_general(left, right, (((left_dim,), (right_dim,)), ((), ())), pre...  37 us
    reduce_scatter x1, waiting for transfers between devices, on_device(): lax.psum_scatter(contract(partner, grad_tok, 0, 0).astype(jnp.bfloat16),...  30 us
    all_to_all x1, blocking collectives, on_device(): lax.all_to_all(attended_rows, ('branch', 'seq'), split_axis=0, concat_axi...  20.5 us
    all_to_all x1, blocking collectives, on_device(): lax.all_to_all(back_rows[1], ('branch', 'seq'), split_axis=0, concat_axis...  19.9 us
    all_to_all x1, blocking collectives, on_device(): lax.all_to_all(back_rows[0], ('branch', 'seq'), split_axis=0, concat_axis...  19.4 us
    all_to_all x1, blocking collectives, on_device(): lax.all_to_all(grad_attended, ('branch', 'seq'), split_axis=1, concat_axi...  18.9 us
  transfers between devices with their start and end apart: 9, of which 9 were waited for; matrix products, arithmetic and copies ran while one was open for 15% of the time, Pallas kernels for 0%

commit v1 on v0

--- a/solution.py
+++ b/solution.py
@@ -98,7 +98,9 @@
     attended = lax.all_to_all(
         attended_rows, ("branch", "seq"), split_axis=0, concat_axis=1, tiled=True
     )
-    proj_own = lax.all_gather(out_proj, "seq", axis=1, tiled=True)[0]
+    proj_own = jnp.concatenate(
+        lax.all_to_all(jnp.stack([out_proj] * lax.axis_size("seq")), "seq", 0, 0), axis=1
+    )[0]
     summed = hidden_in[0].astype(jnp.float32) + grouped_product(attended, proj_own, group_count)
     hidden = lax.optimization_barrier(summed.astype(jnp.bfloat16))
     partner = swapped(hidden, "branch", 0)

time: 395 us -> 371 us (0.939)
  waiting for transfers between devices: 209 us -> 178 us
  local copies, waits for them, and re-layouts: 13.9 us -> 18.2 us
    all_to_all x0 -> x1, waiting for transfers between devices: none -> 112 us  [on_device(): lax.all_to_all(jnp.stack([out_proj] * lax.axis_size('seq')), 'seq', 0, 0)]
    all_gather x1, waiting for transfers between devices: 96.6 us -> 0.02 us  [on_device(): couple_full = lax.all_gather(couple_proj, 'seq', axis=1, tiled=True)[0]]
    all_gather x1 -> x0, waiting for transfers between devices: 43.9 us -> none  [on_device(): proj_own = lax.all_gather(out_proj, 'seq', axis=1, tiled=True)[0]]
    all_to_all x0 -> x1, starting transfers between devices: none -> 4.95 us  [on_device(): lax.all_to_all(jnp.stack([out_proj] * lax.axis_size('seq')), 'seq', 0, 0)]
    another operation x4 -> x5, local copies, waits for them, and re-layouts: 1.86 us -> 6.16 us  [the longest x1 4.3 us: on_device(): jnp.stack([out_proj] * lax.axis_size('seq'))]
  transfers between devices with their start and end apart: 9 -> 9, of which waited for: 9 -> 8; matrix products, arithmetic and copies ran while one was open for 15% -> 17% of each run, Pallas kernels for 0% -> 0%
where the time goes in v1:
time: 371 us; the launch traced here: 370 us
  waiting for transfers between devices  178 us (48%)
  blocking collectives  77.4 us (21%)
  matrix products  42 us (11%)
  starting transfers between devices  30.5 us (8%)
  local copies, waits for them, and re-layouts  18.2 us (5%)
  between operations  14.2 us (4%)
  other arithmetic  9.85 us (3%)
    all_to_all x1, waiting for transfers between devices, on_device(): lax.all_to_all(jnp.stack([out_proj] * lax.axis_size('seq')), 'seq', 0, 0)  112 us
    dot_general x18, matrix products, contract(): lax.dot_general(left, right, (((left_dim,), (right_dim,)), ((), ())), pre...  37.3 us
    reduce_scatter x1, waiting for transfers between devices, on_device(): lax.psum_scatter(contract(partner, grad_tok, 0, 0).astype(jnp.bfloat16),...  27.9 us
    all_to_all x1, blocking collectives, on_device(): lax.all_to_all(back_rows[1], ('branch', 'seq'), split_axis=0, concat_axis...  21 us
    all_to_all x1, blocking collectives, on_device(): lax.all_to_all(back_rows[0], ('branch', 'seq'), split_axis=0, concat_axis...  20.8 us
    all_to_all x1, blocking collectives, on_device(): lax.all_to_all(attended_rows, ('branch', 'seq'), split_axis=0, concat_axi...  20.5 us
    all_to_all x1, blocking collectives, on_device(): lax.all_to_all(grad_attended, ('branch', 'seq'), split_axis=1, concat_axi...  15 us
    all_to_all x1, waiting for transfers between devices, on_device(): lax.all_to_all(key_vecs[0], ('branch', 'seq'), split_axis=1, concat_axis=...  14.1 us
  transfers between devices with their start and end apart: 9, of which 8 were waited for; matrix products, arithmetic and copies ran while one was open for 17% of the time, Pallas kernels for 0%

profile of v1, /device:TPU:1, one launch (start us, length us, event | category | flops | bytes accessed | tf_op | source)
XLA Modules:
  0.0 370.3 jit_solution(7843057023226848136)
XLA Ops:
  7.2 0.7 all-gather.2.cloned.1.call-update
  7.9 1.1 copy.57
  9.1 0.9 copy.43
  10.0 8.4 %all-to-all-start = ((bf16[128,16,128]{2,0,1:T(8,128)(2,1)}), bf16[128,16,128]{2,0,1:T(8,128)(2,1)S(1)}, u32[]{:S(2)}, u32[]{:S(2)}) async-start(bf16[128,16,128]{2,0,1:T(8,128)(2,1)} %copy.43), calls=%async_computation | async-start | bytes 1048576 | tf_op jit(solution)/shard_map/all_to_all | solution.py:86
  18.6 0.9 copy.44
  19.5 9.0 %all-to-all-done = bf16[128,16,128]{2,0,1:T(8,128)(2,1)S(1)} async-done(((bf16[128,16,128]{2,0,1:T(8,128)(2,1)}), bf16[128,16,128]{2,0,1:T(8,128)(2,1)S(1)}, u32[]{:S(2)}, u32[]{:S(2)}) %all-to-all-start) | async-done | bytes 524320 | tf_op jit(solution)/shard_map/all_to_all | solution.py:86
  28.5 5.2 %all-to-all-start.1 = ((bf16[128,16,128]{2,0,1:T(8,128)(2,1)}), bf16[128,16,128]{2,0,1:T(8,128)(2,1)S(1)}, u32[]{:S(2)}, u32[]{:S(2)}) async-start(bf16[128,16,128]{2,0,1:T(8,128)(2,1)} %copy.44), calls=%async_computation.1 | async-start | bytes 1048576 | tf_op jit(solution)/shard_map/all_to_all | solution.py:87
  33.9 0.9 copy.45
  34.8 14.1 %all-to-all-done.1 = bf16[128,16,128]{2,0,1:T(8,128)(2,1)S(1)} async-done(((bf16[128,16,128]{2,0,1:T(8,128)(2,1)}), bf16[128,16,128]{2,0,1:T(8,128)(2,1)S(1)}, u32[]{:S(2)}, u32[]{:S(2)}) %all-to-all-start.1) | async-done | bytes 524320 | tf_op jit(solution)/shard_map/all_to_all | solution.py:87
  48.9 5.0 %all-to-all-start.2 = ((bf16[128,16,128]{2,0,1:T(8,128)(2,1)}), bf16[128,16,128]{2,0,1:T(8,128)(2,1)S(1)}, u32[]{:S(2)}, u32[]{:S(2)}) async-start(bf16[128,16,128]{2,0,1:T(8,128)(2,1)} %copy.45), calls=%async_computation.2 | async-start | bytes 1048576 | tf_op jit(solution)/shard_map/all_to_all | solution.py:88
  53.9 10.1 %all-to-all-done.2 = bf16[128,16,128]{2,0,1:T(8,128)(2,1)S(1)} async-done(((bf16[128,16,128]{2,0,1:T(8,128)(2,1)}), bf16[128,16,128]{2,0,1:T(8,128)(2,1)S(1)}, u32[]{:S(2)}, u32[]{:S(2)}) %all-to-all-start.2) | async-done | bytes 524320 | tf_op jit(solution)/shard_map/all_to_all | solution.py:88
  64.1 5.5 %while.24 = (s32[]{:T(128)}, bf16[2,1024,128]{2,1,0:T(8,128)(2,1)S(1)}, bf16[2,1024,128]{2,1,0:T(8,128)(2,1)S(1)}, bf16[2,1024,128]{2,1,0:T(8,128)(2,1)S(1)}, bf16[2,1024,128]{2,1,0:T(8,128)(2,1)S(1)}, /*index=5*/s32[]{:T(128)}) while((s32[]{:T(128)}, bf16[2,1024,128]{2,1,0:T(8,128)(2,1)S(1)}, bf16[2,1024,128]{2,1,0:T(8,128)(2,1)S(1)}, ...), condition=%wide.region_3.4_spmd, body=%wide.region_0.3_spmd.sunk | while | flops 546437120 | bytes 13654085 | solution.py:94
  64.1 0.7 multiply_reduce_fusion.6
  64.8 0.7 fusion.102
  65.6 1.2 fusion.103
  66.8 0.7 multiply_reduce_fusion.6
  67.5 0.7 fusion.102
  68.3 1.3 fusion.103
  69.6 0.8 copy-done.9
  70.4 20.5 %all_to_all.133 = bf16[16,128,128]{2,1,0:T(8,128)(2,1)S(1)} all-to-all(bf16[16,128,128]{2,1,0:T(8,128)(2,1)S(1)} %bitcast.180), channel_id=1, replica_groups=mesh['branch'=2,'seq'=8,'rep'=16] {'branch','seq'}, dimensions={0} | all-to-all | bytes 1048576 | tf_op jit(solution)/shard_map/all_to_all | solution.py:98
  90.9 4.3 %stack.2 = bf16[8,1,256,2048]{3,2,1,0:T(8,128)(2,1)} broadcast(bf16[256,2048]{1,0:T(8,128)(2,1)S(1)} %bitcast.188), dimensions={2,3} | broadcast | bytes 9437184 | tf_op jit(solution)/shard_map/stack | solution.py:102
  95.2 5.0 %all-to-all-start.4 = ((bf16[8,1,256,2048]{3,2,1,0:T(8,128)(2,1)}), bf16[8,1,256,2048]{3,2,1,0:T(8,128)(2,1)}, u32[]{:S(2)}, u32[]{:S(2)}) async-start(bf16[8,1,256,2048]{3,2,1,0:T(8,128)(2,1)} %stack.2), calls=%async_computation.4 | async-start | bytes 16777216 | tf_op jit(solution)/shard_map/all_to_all | solution.py:102
  100.5 112.0 %all-to-all-done.4 = bf16[8,1,256,2048]{3,2,1,0:T(8,128)(2,1)} async-done(((bf16[8,1,256,2048]{3,2,1,0:T(8,128)(2,1)}), bf16[8,1,256,2048]{3,2,1,0:T(8,128)(2,1)}, u32[]{:S(2)}, u32[]{:S(2)}) %all-to-all-start.4) | async-done | bytes 8388640 | tf_op jit(solution)/shard_map/all_to_all | solution.py:102
  212.5 4.7 %fusion.62 = bf16[8,128,2048]{2,1,0:T(8,128)(2,1)S(1)} fusion(bf16[128,8,256]{0,2,1:T(8,128)(2,1)S(1)} %bitcast.175, bf16[8,1,256,2048]{3,2,1,0:T(8,128)(2,1)} %all-to-all-done.4), kind=kOutput, calls=%fused_computation.66 | convolution fusion | flops 1075838976 | bytes 13107200 | tf_op jit(solution)/shard_map/dot_general | solution.py:73
  217.2 0.7 convert_reduce_fusion
  218.4 0.8 copy-done.5
  219.2 0.8 collective-permute-start
  220.0 1.5 collective-permute-done
  221.5 5.6 %convolution_convert_fusion = bf16[2048,2048]{1,0:T(8,128)(2,1)} fusion(bf16[128,2048]{1,0:T(8,128)(2,1)S(1)} %collective-permute-done, bf16[1,128,2048]{2,1,0:T(8,128)(2,1)S(1)} %copy-done), kind=kOutput, calls=%fused_computation.65 | convolution fusion | flops 1077936128 | bytes 9437184 | tf_op jit(solution)/shard_map/dot_general | solution.py:17
  227.2 6.3 %fusion.68 = bf16[128,2048]{1,0:T(8,128)(2,1)S(1)} fusion(bf16[1,2048,2048]{2,1,0:T(8,128)(2,1)} %all-gather.2.cloned.1.call-done, bf16[1,128,2048]{2,1,0:T(8,128)(2,1)S(1)} %copy-done), kind=kOutput, calls=%fused_computation.68 | convolution fusion | flops 1074003968 | bytes 9437184 | tf_op jit(solution)/shard_map/dot_general | solution.py:17
  233.4 0.5 collective-permute-start.1
  233.9 1.5 collective-permute-done.1
  235.4 7.0 %fusion.77 = bf16[16,16,8,128]{3,2,1,0:T(8,128)(2,1)S(1)} fusion(bf16[2048,2048]{1,0:T(8,128)(2,1)} %bitcast.29, bf16[128,2048]{1,0:T(8,128)(2,1)S(1)} %collective-permute-done.1, bf16[1,128,2048]{2,1,0:T(8,128)(2,1)S(1)} %copy-done), kind=kOutput, calls=%fused_computation.72 | convolution fusion | flops 1075052544 | bytes 9961472 | tf_op jit(solution)/shard_map/dot_general | solution.py:17
  242.6 15.0 %all_to_all.136 = bf16[128,16,128]{2,0,1:T(8,128)(2,1)} all-to-all(bf16[128,16,128]{2,0,1:T(8,128)(2,1)S(1)} %bitcast.181), channel_id=1, replica_groups=mesh['branch'=2,'seq'=8,'rep'=16] {'branch','seq'}, dimensions={1} | all-to-all | bytes 1048576 | tf_op jit(solution)/shard_map/all_to_all | solution.py:118
  257.6 0.9 broadcast.20.clone.2
  258.5 0.9 broadcast.20.clone.3
  259.4 14.7 %while.25 = (s32[]{:T(128)}, bf16[2,1024,128]{2,1,0:T(8,128)(2,1)S(1)}, bf16[2,1024,128]{2,1,0:T(8,128)(2,1)}, bf16[2,1024,128]{2,1,0:T(8,128)(2,1)}, bf16[2,102...) while((s32[]{:T(128)}, ...), condition=%wide.region_9.10_spmd, body=%wide.region_5.9_spmd.sunk | while | flops 1363801088 | bytes 50906372 | solution.py:127
  259.4 0.7 multiply_reduce_fusion.7
  260.1 0.7 fusion.110
  260.8 1.0 fusion.113
  261.9 1.1 multiply_reduce_fusion.8
  263.0 1.2 multiply_convert_fusion.2
  264.2 0.8 fusion.112
  265.1 0.8 copy-done.2
  265.8 0.9 fusion.111
  266.8 0.7 multiply_reduce_fusion.7
  267.5 0.7 fusion.110
  268.2 1.0 fusion.113
  269.3 1.1 multiply_reduce_fusion.8
  270.4 1.2 multiply_convert_fusion.2
  271.6 0.8 fusion.112
  272.4 0.8 copy-done.2
  273.2 0.9 fusion.111
  274.1 20.8 %all_to_all.134 = bf16[16,128,128]{2,1,0:T(8,128)(2,1)S(1)} all-to-all(bf16[16,128,128]{2,1,0:T(8,128)(2,1)S(1)} %bitcast.176), channel_id=1, replica_groups=mesh['branch'=2,'seq'=8,'rep'=16] {'branch','seq'}, dimensions={0} | all-to-all | bytes 1048576 | tf_op jit(solution)/shard_map/all_to_all | solution.py:137
  294.9 21.0 %all_to_all.135 = bf16[16,128,128]{2,1,0:T(8,128)(2,1)S(1)} all-to-all(bf16[16,128,128]{2,1,0:T(8,128)(2,1)} %bitcast.177), channel_id=1, replica_groups=mesh['branch'=2,'seq'=8,'rep'=16] {'branch','seq'}, dimensions={0} | all-to-all | bytes 1048576 | tf_op jit(solution)/shard_map/all_to_all | solution.py:138
  316.0 5.5 %all-to-all-start.8 = ((bf16[16,128,128]{2,1,0:T(8,128)(2,1)}), bf16[16,128,128]{2,1,0:T(8,128)(2,1)S(1)}, u32[]{:S(2)}, u32[]{:S(2)}) async-start(bf16[16,128,128]{2,1,0:T(8,128)(2,1)} %bitcast.178), calls=%async_computation.8 | async-start | bytes 1048576 | tf_op jit(solution)/shard_map/all_to_all | solution.py:139
  321.4 5.5 %fusion.74 = bf16[1,128,2048]{2,1,0:T(8,128)(2,1)} fusion(bf16[128,2048]{1,0:T(8,128)(2,1)S(1)} %collective-permute-done, bf16[1,2048,2048]{2,1,0:T(8,128)(2,1)} %all-gather.2.cloned.1.call-done, bf16[128,2048]{1,0:T(8,128)(2,1)} %copy-done.5), kind=kOutput, calls=%fused_computation.71 | convolution fusion | flops 1074528256 | bytes 9961472 | tf_op jit(solution)/shard_map/dot_general | solution.py:17
  326.9 0.9 fusion.81
  328.1 1.0 copy.52
  329.4 1.0 copy.53
  330.4 1.1 all-to-all-done.8
  331.8 1.0 copy.54
  332.8 27.9 %reduce-scatter.2.cloned.1.call-done = bf16[256,2048]{1,0:T(8,128)(2,1)} async-done(((bf16[2048,2048]{1,0:T(8,128)(2,1)}), bf16[256,2048]{1,0:T(8,128)(2,1)}) %reduce-scatter.2.cloned.1.call-update) | async-done | bytes 1048592 | tf_op jit(solution)/shard_map/reduce_scatter | solution.py:121
  360.7 2.8 bitcast_convert_fusion
  (48 shorter events, 2.2 us)
Async XLA Ops:
  7.2 11.3 %copy-start.7 = (bf16[1,128,2048]{2,1,0:T(8,128)(2,1)S(1)}, bf16[1,128,2048]{2,1,0:T(8,128)(2,1)}, u32[]{:S(2)}) copy-start(bf16[1,128,2048]{2,1,0:T(8,128)(2,1)} %param.12) | copy-start | bytes 1572868
  7.2 26.6 %copy-start.8 = (bf16[1,128,2048]{2,1,0:T(8,128)(2,1)S(1)}, bf16[1,128,2048]{2,1,0:T(8,128)(2,1)}, u32[]{:S(2)}) copy-start(bf16[1,128,2048]{2,1,0:T(8,128)(2,1)} %param.13) | copy-start | bytes 1572868
  7.2 220.0 %all-gather.2.cloned.1.call-start = ((), (), s32[]{:S(2)}) async-start(), calls=%async_computation.10 | async-start | bytes 9437184 | tf_op jit(solution)/shard_map/all_gather | solution.py:107
  10.0 18.5 %all-to-all-start = ((bf16[128,16,128]{2,0,1:T(8,128)(2,1)}), bf16[128,16,128]{2,0,1:T(8,128)(2,1)S(1)}, u32[]{:S(2)}, u32[]{:S(2)}) async-start(bf16[128,16,128]{2,0,1:T(8,128)(2,1)} %copy.43), calls=%async_computation | async-start | bytes 1048576 | tf_op jit(solution)/shard_map/all_to_all | solution.py:86
  28.5 20.4 %all-to-all-start.1 = ((bf16[128,16,128]{2,0,1:T(8,128)(2,1)}), bf16[128,16,128]{2,0,1:T(8,128)(2,1)S(1)}, u32[]{:S(2)}, u32[]{:S(2)}) async-start(bf16[128,16,128]{2,0,1:T(8,128)(2,1)} %copy.44), calls=%async_computation.1 | async-start | bytes 1048576 | tf_op jit(solution)/shard_map/all_to_all | solution.py:87
  48.9 15.1 %all-to-all-start.2 = ((bf16[128,16,128]{2,0,1:T(8,128)(2,1)}), bf16[128,16,128]{2,0,1:T(8,128)(2,1)S(1)}, u32[]{:S(2)}, u32[]{:S(2)}) async-start(bf16[128,16,128]{2,0,1:T(8,128)(2,1)} %copy.45), calls=%async_computation.2 | async-start | bytes 1048576 | tf_op jit(solution)/shard_map/all_to_all | solution.py:88
  64.1 26.8 %copy-start.6 = (bf16[1,256,2048]{2,1,0:T(8,128)(2,1)S(1)}, bf16[1,256,2048]{2,1,0:T(8,128)(2,1)}, u32[]{:S(2)}) copy-start(bf16[1,256,2048]{2,1,0:T(8,128)(2,1)} %param.15) | copy-start | bytes 3145732
  69.6 0.8 copy-start.9
  95.2 117.3 %all-to-all-start.4 = ((bf16[8,1,256,2048]{3,2,1,0:T(8,128)(2,1)}), bf16[8,1,256,2048]{3,2,1,0:T(8,128)(2,1)}, u32[]{:S(2)}, u32[]{:S(2)}) async-start(bf16[8,1,256,2048]{3,2,1,0:T(8,128)(2,1)} %stack.2), calls=%async_computation.4 | async-start | bytes 16777216 | tf_op jit(solution)/shard_map/all_to_all | solution.py:102
  100.1 260.5 %reduce-scatter.2.cloned.1.call-start = ((), (), s32[]{:S(2)}) async-start(), calls=%async_computation.11 | async-start | bytes 9437184 | tf_op jit(solution)/shard_map/reduce_scatter | solution.py:121
  217.2 1.0 copy-start.12
  217.2 4.3 %copy-start = (bf16[1,128,2048]{2,1,0:T(8,128)(2,1)S(1)}, bf16[1,128,2048]{2,1,0:T(8,128)(2,1)}, u32[]{:S(2)}) copy-start(bf16[1,128,2048]{2,1,0:T(8,128)(2,1)} %param.17) | copy-start | bytes 1572868
  218.4 0.8 copy-start.5
  219.2 2.3 collective-permute-start
  233.4 2.0 collective-permute-start.1
  259.4 1.5 copy-start.3
  259.4 1.5 copy-start.11
  260.8 1.1 copy-start.10
  261.9 1.1 copy-start.4
  263.0 1.2 copy-start.1
  265.1 0.8 copy-start.2
  266.7 1.5 copy-start.3
  266.7 1.5 copy-start.11
  268.2 1.1 copy-start.10
  269.3 1.1 copy-start.4
  270.4 1.2 copy-start.1
  272.4 0.8 copy-start.2
  316.0 15.5 %all-to-all-start.8 = ((bf16[16,128,128]{2,1,0:T(8,128)(2,1)}), bf16[16,128,128]{2,1,0:T(8,128)(2,1)S(1)}, u32[]{:S(2)}, u32[]{:S(2)}) async-start(bf16[16,128,128]{2,1,0:T(8,128)(2,1)} %bitcast.178), calls=%async_computation.8 | async-start | bytes 1048576 | tf_op jit(solution)/shard_map/all_to_all | solution.py:139
Sparse Core Ops, SparseCore 0:
  10.6 195.1 all-gather.1
  227.3 133.3 reduce-scatter.1
